TPU v7x, 256 devices: a whole 4x4x8 slice. The times are simulated.
256 devices in a mesh: pipe: 4 (over x), seq: 64 (over y, z, core).
Axes of the slice: x: 4, y: 4, z: 8, core: 2. Of those that a mesh axis runs over, the one named last changes fastest.
Arguments:
- arriving: bfloat16 [4, 65536, 2048], P('pipe', 'seq'), may hold values from -6 to 6
- loss_grad: bfloat16 [65536, 2048], P('seq', 'pipe'), may hold values from -6 to 6
- first_blocks: bfloat16 [4, 256, 256, 256], P('pipe', 'seq'), may hold values from -0.375 to 0.375
- second_blocks: bfloat16 [4, 256, 256, 256], P('pipe', 'seq'), may hold values from -0.375 to 0.375
- inner_gain: bfloat16 [4, 2048], P('pipe'), may hold values from 0.25 to 1.75
- outer_gain: bfloat16 [4, 2048], P('pipe'), may hold values from 0.25 to 1.75
Outputs:
- entering: bfloat16 [4, 65536, 2048], P('pipe', 'seq')
- leaving: bfloat16 [65536, 2048], P('seq', 'pipe')
All inputs are finite; a program needn't handle non-finite values.
Results may differ from a plain program's by a relative error of at most 0.0059.
Values may be sent and summed in bfloat16 or wider, within the bound.
No kernel may reach another device: no remote copies, remote signals or barrier semaphores. Data moves between devices by JAX's collectives and lax.ppermute only.
A program may use at most 128 MiB of HBM per device.

v0:
```python
import jax
import jax.numpy as jnp
from jax import lax
from jax.sharding import PartitionSpec as P


def shifted(block, axis, distance):
    devices = range(lax.axis_size(axis))
    route = [((i - distance) % len(devices), i) for i in devices]
    return lax.ppermute(block, axis, route)


def from_root(array, axis, root):
    mine = lax.axis_index(axis) == root
    return lax.psum(jnp.where(mine, array, jnp.zeros_like(array)), axis)


def mixer(gradient, first_part, second_part, inner_part, outer_part):
    row_count = first_part.shape[0]
    block_order = first_part.shape[1]
    blocked = gradient.reshape(row_count, block_order, gradient.shape[1]).astype(jnp.float32)
    scaled = (blocked * inner_part.astype(jnp.float32)).astype(jnp.bfloat16)
    mixed = jnp.einsum(
        "kjc,jki->ijc",
        lax.all_to_all(scaled, "seq", split_axis=1, concat_axis=0, tiled=True),
        second_part,
        preferred_element_type=jnp.float32,
    ).astype(jnp.bfloat16)
    returned = lax.all_to_all(mixed, "seq", split_axis=0, concat_axis=1, tiled=True)
    spread = jnp.einsum("ikc,ikj->ijc", returned, first_part, preferred_element_type=jnp.float32)
    result = blocked + outer_part.astype(jnp.float32) * spread
    return result.astype(jnp.bfloat16).reshape(gradient.shape)


def per_device(arriving, loss_grad, first_blocks, second_blocks, inner_gain, outer_gain):
    sections = lax.axis_size("pipe")
    position = lax.axis_index("pipe")
    whole_loss = lax.all_gather(loss_grad, "pipe", axis=1, tiled=True)
    own_result = mixer(arriving[0], first_blocks[0], second_blocks[0], inner_gain[0], outer_gain[0])
    passed = shifted(own_result, "pipe", -1)
    exit_root = sections - 1
    source = jnp.where(position == sections - 1, whole_loss, passed)
    entering = mixer(source, first_blocks[0], second_blocks[0], inner_gain[0], outer_gain[0])
    copied = from_root(passed, "pipe", exit_root)
    channel_width = loss_grad.shape[1]
    leaving = lax.dynamic_slice_in_dim(copied, position * channel_width, channel_width, 1)
    return (entering[None], leaving)


def solution(mesh):
    placed = (
        P("pipe", "seq", None),
        P("seq", "pipe"),
        P("pipe", "seq", None, None),
        P("pipe", "seq", None, None),
        P("pipe", None),
        P("pipe", None),
    )
    return jax.shard_map(
        per_device,
        mesh=mesh,
        in_specs=placed,
        out_specs=(P("pipe", "seq", None), P("seq", "pipe")),
        check_vma=False,
    )
```

profile of v0, /device:TPU:1, one launch (start us, length us, event | category | flops | bytes accessed | tf_op | source)
XLA Modules:
  0.0 639.2 jit_solution(10214228244827802752)
XLA Ops:
  7.9 3.3 fusion
  11.2 3.2 copy.24
  14.5 109.1 %all_to_all.72 = bf16[4,256,2048]{2,0,1:T(4,128)(2,1)S(1)} all-to-all(bf16[4,256,2048]{2,0,1:T(4,128)(2,1)S(1)} %copy.24), channel_id=1, replica_groups=mesh['pipe'=4,'seq'=64] {'seq'}, dimensions={1} | all-to-all | bytes 8388608 | tf_op jit(solution)/shard_map/all_to_all | solution.py:25
  123.6 8.3 %copy.25 = bf16[4,64,4,2048]{3,2,0,1:T(4,128)(2,1)S(1)} copy(bf16[4,64,4,2048]{3,0,2,1:T(4,128)(2,1)S(1)} %bitcast.44) | data formatting | bytes 8388608 | tf_op jit(solution)/shard_map/all_to_all | solution.py:25
  131.9 7.7 %convert_bitcast_fusion.1 = bf16[256,4,2048]{0,2,1:T(8,128)(2,1)} fusion(bf16[256,4,2048]{2,1,0:T(4,128)(2,1)S(1)} %bitcast.45, bf16[1,4,256,256]{3,2,1,0:T(8,128)(2,1)S(1)} %copy-done), kind=kOutput, calls=%fused_computation.13 | convolution fusion | flops 1075838976 | bytes 8912896 | tf_op jit(solution)/shard_map/kjc,jki->ijc/dot_general | solution.py:23
  139.6 7.9 %copy.27 = bf16[256,4,2048]{2,1,0:T(4,128)(2,1)} copy(bf16[256,4,2048]{0,2,1:T(8,128)(2,1)} %convert_bitcast_fusion.1) | data formatting | bytes 8388608 | tf_op jit(solution)/shard_map/convert_element_type | solution.py:28
  147.5 6.2 all-to-all-start.1
  154.4 95.1 %all-to-all-done.1 = bf16[256,4,2048]{2,1,0:T(4,128)(2,1)} async-done(((bf16[256,4,2048]{2,1,0:T(4,128)(2,1)}), bf16[256,4,2048]{2,1,0:T(4,128)(2,1)}, u32[]{:S(2)}, u32[]{:S(2)}) %all-to-all-start.1) | async-done | bytes 4194336 | tf_op jit(solution)/shard_map/all_to_all | solution.py:29
  249.5 7.0 %copy.28 = bf16[4,64,4,2048]{3,2,1,0:T(4,128)(2,1)} copy(bf16[4,64,4,2048]{3,2,0,1:T(4,128)(2,1)} %bitcast.10) | data formatting | bytes 8388608 | tf_op jit(solution)/shard_map/all_to_all | solution.py:29
  256.5 7.0 %all_to_all.59 = bf16[4,256,2048]{2,1,0:T(8,128)(2,1)} reshape(bf16[4,64,4,2048]{3,2,1,0:T(4,128)(2,1)} %copy.28) | data formatting | bytes 8388608 | tf_op jit(solution)/shard_map/all_to_all | solution.py:29
  263.5 6.9 %fusion.1 = bf16[4,256,2048]{2,1,0:T(8,128)(2,1)} fusion(bf16[4,256,2048]{2,1,0:T(8,128)(2,1)} %bitcast.49, bf16[4,256,2048]{2,1,0:T(8,128)(2,1)} %all_to_all.59, f32[2048]{0:T(1024)S(1)} %bitcast.53, bf16[1,4,256,256]{3,2,1,0:T(8,128)(2,1)S(1)} %copy-done.2), kind=kOutput, calls=%fused_computation.5 | convolution fusion | flops 1082130432 | bytes 13115392 | tf_op jit(solution)/shard_map/ikc,ikj->ijc/dot_general | solution.py:30
  270.5 2.5 collective-permute-start
  273.0 90.0 %collective-permute-done = bf16[1024,2048]{1,0:T(8,128)(2,1)} collective-permute-done((bf16[1024,2048]{1,0:T(8,128)(2,1)}, bf16[1024,2048]{1,0:T(8,128)(2,1)}, u32[]{:S(2)}, u32[]{:S(2)}) %collective-permute-start) | collective-permute-done | bytes 4194336 | tf_op jit(solution)/shard_map/ppermute | solution.py:10
  362.9 3.9 broadcast_select_fusion
  369.9 3.2 copy.30
  373.2 101.9 %all_to_all.73 = bf16[4,256,2048]{2,0,1:T(4,128)(2,1)S(1)} all-to-all(bf16[4,256,2048]{2,0,1:T(4,128)(2,1)S(1)} %copy.30), channel_id=1, replica_groups=mesh['pipe'=4,'seq'=64] {'seq'}, dimensions={1} | all-to-all | bytes 8388608 | tf_op jit(solution)/shard_map/all_to_all | solution.py:25
  475.1 8.3 %copy.31 = bf16[4,64,4,2048]{3,2,0,1:T(4,128)(2,1)S(1)} copy(bf16[4,64,4,2048]{3,0,2,1:T(4,128)(2,1)S(1)} %bitcast.46) | data formatting | bytes 8388608 | tf_op jit(solution)/shard_map/all_to_all | solution.py:25
  483.4 7.5 %convert_bitcast_fusion = bf16[256,4,2048]{0,2,1:T(8,128)(2,1)} fusion(bf16[256,4,2048]{2,1,0:T(4,128)(2,1)S(1)} %bitcast.47, bf16[1,4,256,256]{3,2,1,0:T(8,128)(2,1)S(1)} %copy-done), kind=kOutput, calls=%fused_computation.12 | convolution fusion | flops 1075838976 | bytes 8912896 | tf_op jit(solution)/shard_map/kjc,jki->ijc/dot_general | solution.py:23
  490.8 8.0 %copy.33 = bf16[256,4,2048]{2,1,0:T(4,128)(2,1)} copy(bf16[256,4,2048]{0,2,1:T(8,128)(2,1)} %convert_bitcast_fusion) | data formatting | bytes 8388608 | tf_op jit(solution)/shard_map/convert_element_type | solution.py:28
  498.8 6.0 all-to-all-start.3
  505.6 103.4 %all-reduce.2.cloned.1.call-done = bf16[1024,2048]{1,0:T(8,128)(2,1)} async-done(((bf16[1024,2048]{1,0:T(8,128)(2,1)}), bf16[1024,2048]{1,0:T(8,128)(2,1)}) %all-reduce.2.cloned.1.call-update) | async-done | bytes 4194320 | tf_op jit(solution)/shard_map/psum | solution.py:15
  611.2 7.0 %copy.34 = bf16[4,64,4,2048]{3,2,1,0:T(4,128)(2,1)} copy(bf16[4,64,4,2048]{3,2,0,1:T(4,128)(2,1)} %bitcast.21) | data formatting | bytes 8388608 | tf_op jit(solution)/shard_map/all_to_all | solution.py:29
  618.2 6.9 %all_to_all.67 = bf16[4,256,2048]{2,1,0:T(8,128)(2,1)} reshape(bf16[4,64,4,2048]{3,2,1,0:T(4,128)(2,1)} %copy.34) | data formatting | bytes 8388608 | tf_op jit(solution)/shard_map/all_to_all | solution.py:29
  625.2 6.9 %fusion.3 = bf16[4,256,2048]{2,1,0:T(8,128)(2,1)} fusion(bf16[4,256,2048]{2,1,0:T(8,128)(2,1)} %bitcast.43, bf16[4,256,2048]{2,1,0:T(8,128)(2,1)} %all_to_all.67, f32[2048]{0:T(1024)S(1)} %bitcast.54, bf16[1,4,256,256]{3,2,1,0:T(8,128)(2,1)S(1)} %copy-done.2), kind=kOutput, calls=%fused_computation.7 | convolution fusion | flops 1082130432 | bytes 13115392 | tf_op jit(solution)/shard_map/ikc,ikj->ijc/dot_general | solution.py:30
  (18 shorter events, 7.6 us)
Async XLA Ops:
  7.2 124.7 %copy-start = (bf16[1,4,256,256]{3,2,1,0:T(8,128)(2,1)S(1)}, bf16[1,4,256,256]{3,2,1,0:T(8,128)(2,1)}, u32[]{:S(2)}) copy-start(bf16[1,4,256,256]{3,2,1,0:T(8,128)(2,1)} %param.9) | copy-start | bytes 1572868
  147.5 6.9 %copy-start.3 = (bf16[1,2048]{1,0:T(2,128)(2,1)S(1)}, bf16[1,2048]{1,0:T(2,128)(2,1)}, u32[]{:S(2)}) copy-start(bf16[1,2048]{1,0:T(2,128)(2,1)} %param.11) | copy-start | bytes 12292
  147.5 102.0 %all-to-all-start.1 = ((bf16[256,4,2048]{2,1,0:T(4,128)(2,1)}), bf16[256,4,2048]{2,1,0:T(4,128)(2,1)}, u32[]{:S(2)}, u32[]{:S(2)}) async-start(bf16[256,4,2048]{2,1,0:T(4,128)(2,1)} %copy.27), calls=%async_computation.1 | async-start | bytes 8388608 | tf_op jit(solution)/shard_map/all_to_all | solution.py:29
  153.7 119.3 %all-gather.2.cloned.1.call-start = ((), (), s32[]{:S(2)}) async-start(), calls=%async_computation.4 | async-start | bytes 5242880 | tf_op jit(solution)/shard_map/all_gather | solution.py:38
  256.5 7.0 %copy-start.2 = (bf16[1,4,256,256]{3,2,1,0:T(8,128)(2,1)S(1)}, bf16[1,4,256,256]{3,2,1,0:T(8,128)(2,1)}, u32[]{:S(2)}) copy-start(bf16[1,4,256,256]{3,2,1,0:T(8,128)(2,1)} %param.8) | copy-start | bytes 1572868
  270.5 92.5 %collective-permute-start = (bf16[1024,2048]{1,0:T(8,128)(2,1)}, bf16[1024,2048]{1,0:T(8,128)(2,1)}, u32[]{:S(2)}, u32[]{:S(2)}) collective-permute-start(bf16[1024,2048]{1,0:T(8,128)(2,1)} %bitcast.13), channel_id=1, source_target_pairs={{64,0},{128,64},{192,128},{0,192},{65,1},{129,65},{193,129},{1,193... | collective-permute-start | bytes 12582920 | tf_op jit(solution)/shard_map/ppermute | solution.py:10
  366.8 1.9 copy-start.1
  498.8 112.4 %all-to-all-start.3 = ((bf16[256,4,2048]{2,1,0:T(4,128)(2,1)}), bf16[256,4,2048]{2,1,0:T(4,128)(2,1)}, u32[]{:S(2)}, u32[]{:S(2)}) async-start(bf16[256,4,2048]{2,1,0:T(4,128)(2,1)} %copy.33), calls=%async_computation.3 | async-start | bytes 8388608 | tf_op jit(solution)/shard_map/all_to_all | solution.py:29
  504.8 104.1 %all-reduce.2.cloned.1.call-start = ((), (), s32[]{:S(2)}) async-start(), calls=%async_computation.5 | async-start | bytes 8388608 | tf_op jit(solution)/shard_map/psum | solution.py:15
Sparse Core Ops, SparseCore 0:
  156.3 51.5 all-gather.1
  508.6 100.3 all-reduce.1
where the time goes:
time: 645 us; the launch traced here: 639 us
  waiting for transfers between devices  290 us (45%)
  blocking collectives  211 us (33%)
  local copies, waits for them, and re-layouts  71.2 us (11%)
  matrix products  29 us (4%)
  starting transfers between devices  14.7 us (2%)
  between operations  14.4 us (2%)
  other arithmetic  9.1 us (1%)
    all_to_all x2, blocking collectives, mixer(): lax.all_to_all(scaled, 'seq', split_axis=1, concat_axis=0, tiled=True)  211 us
    psum x1, waiting for transfers between devices, from_root(): return lax.psum(jnp.where(mine, array, jnp.zeros_like(array)), axis)  103 us
    all_to_all x2, waiting for transfers between devices, mixer(): lax.all_to_all(mixed, 'seq', split_axis=0, concat_axis=1, tiled=True)  95.1 us
    ppermute x1, waiting for transfers between devices, shifted(): return lax.ppermute(block, axis, route)  90 us
    all_to_all x4, local copies, waits for them, and re-layouts, mixer(): lax.all_to_all(mixed, 'seq', split_axis=0, concat_axis=1, tiled=True)  27.9 us
    all_to_all x2, local copies, waits for them, and re-layouts, mixer(): lax.all_to_all(scaled, 'seq', split_axis=1, concat_axis=0, tiled=True)  16.6 us
    convert_element_type x2, local copies, waits for them, and re-layouts, mixer(): mixed = jnp.einsum('kjc,jki->ijc', lax.all_to_all(scaled, 'seq', split_ax...  15.9 us
    dot_general x2, matrix products, mixer(): jnp.einsum('kjc,jki->ijc', lax.all_to_all(scaled, 'seq', split_axis=1, co...  15.2 us
  transfers between devices with their start and end apart: 5, of which 3 were waited for; matrix products, arithmetic and copies ran while one was open for 3% of the time, Pallas kernels for 0%

commit v1 on v0

--- a/solution.py
+++ b/solution.py
@@ -26,7 +26,9 @@
         second_part,
         preferred_element_type=jnp.float32,
     ).astype(jnp.bfloat16)
-    returned = lax.all_to_all(mixed, "seq", split_axis=0, concat_axis=1, tiled=True)
+    shards = jnp.split(mixed, lax.axis_size("seq"), axis=0)
+    arrived = lax.all_to_all(jnp.stack(shards), "seq", 0, 0)
+    returned = jnp.concatenate(arrived, axis=1)
     spread = jnp.einsum("ikc,ikj->ijc", returned, first_part, preferred_element_type=jnp.float32)
     result = blocked + outer_part.astype(jnp.float32) * spread
     return result.astype(jnp.bfloat16).reshape(gradient.shape)

time: 645 us -> 693 us (1.074)
  local copies, waits for them, and re-layouts: 71.2 us -> 116 us
    unnamed x8 -> x134, local copies, waits for them, and re-layouts: 1.96 us -> 84.1 us
    all_to_all x4 -> x0, local copies, waits for them, and re-layouts: 27.9 us -> none  [mixer(): lax.all_to_all(mixed, 'seq', split_axis=0, concat_axis=1, tiled=True)]
    convert_element_type x2 -> x0, local copies, waits for them, and re-layouts: 15.9 us -> none  [mixer(): mixed = jnp.einsum('kjc,jki->ijc', lax.all_to_all(scaled, 'seq', split_ax...]
    dot_general x2, matrix products: 15.2 us -> 6.96 us  [mixer(): jnp.einsum('kjc,jki->ijc', lax.all_to_all(scaled, 'seq', split_axis=1, co...]
    dot_general x2, matrix products: 13.9 us -> 21.7 us  [mixer(): jnp.einsum('ikc,ikj->ijc', returned, first_part, preferred_element_type=j...]
    all_to_all x2 -> x4, local copies, waits for them, and re-layouts: 16.6 us -> 21.9 us  [mixer(): lax.all_to_all(scaled, 'seq', split_axis=1, concat_axis=0, tiled=True)]
  transfers between devices with their start and end apart: 5 -> 5, of which waited for: 3 -> 3; matrix products, arithmetic and copies ran while one was open for 3% -> 2% of each run, Pallas kernels for 0% -> 0%
where the time goes in v1:
time: 693 us; the launch traced here: 684 us
  waiting for transfers between devices  290 us (42%)
  blocking collectives  211 us (30%)
  local copies, waits for them, and re-layouts  116 us (17%)
  matrix products  28.7 us (4%)
  starting transfers between devices  14.9 us (2%)
  between operations  14.4 us (2%)
  other arithmetic  9.1 us (1%)
    all_to_all x2, blocking collectives, mixer(): lax.all_to_all(scaled, 'seq', split_axis=1, concat_axis=0, tiled=True)  211 us
    psum x1, waiting for transfers between devices, from_root(): return lax.psum(jnp.where(mine, array, jnp.zeros_like(array)), axis)  103 us
    all_to_all x2, waiting for transfers between devices, mixer(): arrived = lax.all_to_all(jnp.stack(shards), 'seq', 0, 0)  95.1 us
    ppermute x1, waiting for transfers between devices, shifted(): return lax.ppermute(block, axis, route)  90 us
    unnamed x134, local copies, waits for them, and re-layouts  84.1 us
    all_to_all x4, local copies, waits for them, and re-layouts, mixer(): lax.all_to_all(scaled, 'seq', split_axis=1, concat_axis=0, tiled=True)  21.9 us
    dot_general x2, matrix products, mixer(): jnp.einsum('ikc,ikj->ijc', returned, first_part, preferred_element_type=j...  21.7 us
  transfers between devices with their start and end apart: 5, of which 3 were waited for; matrix products, arithmetic and copies ran while one was open for 2% of the time, Pallas kernels for 0%

profile of v1, /device:TPU:1, one launch (start us, length us, event | category | flops | bytes accessed | tf_op | source)
XLA Modules:
  0.0 683.8 jit_solution(12270135655021012857)
XLA Ops:
  7.2 0.8 convert_element_type.76
  7.9 3.3 fusion
  11.2 3.2 copy.16
  14.5 109.1 %all_to_all.46 = bf16[4,256,2048]{2,0,1:T(4,128)(2,1)S(1)} all-to-all(bf16[4,256,2048]{2,0,1:T(4,128)(2,1)S(1)} %copy.16), channel_id=1, replica_groups=mesh['pipe'=4,'seq'=64] {'seq'}, dimensions={1} | all-to-all | bytes 8388608 | tf_op jit(solution)/shard_map/all_to_all | solution.py:25
  123.6 4.1 copy.37
  127.7 6.9 %all_to_all.35 = bf16[256,4,2048]{2,0,1:T(8,128)(2,1)} reshape(bf16[64,4,4,2048]{3,1,0,2:T(4,128)(2,1)} %bitcast.561) | data formatting | bytes 8388608 | tf_op jit(solution)/shard_map/all_to_all | solution.py:25
  134.6 3.5 convert_bitcast_fusion.1
  180.1 6.2 all-to-all-start.1
  187.0 95.1 %all-to-all-done.1 = bf16[64,4,4,2048]{3,1,2,0:T(4,128)(2,1)} async-done(((bf16[64,4,4,2048]{3,1,2,0:T(4,128)(2,1)}), bf16[64,4,4,2048]{3,1,2,0:T(4,128)(2,1)}, u32[]{:S(2)}, u32[]{:S(2)}) %all-to-all-start.1) | async-done | bytes 4194336 | tf_op jit(solution)/shard_map/all_to_all | solution.py:30
  282.1 10.9 %fusion.1 = bf16[4,256,2048]{2,1,0:T(8,128)(2,1)} fusion(bf16[4,256,2048]{2,1,0:T(8,128)(2,1)} %bitcast.565, bf16[4,256,2048]{2,0,1:T(4,128)(2,1)} %bitcast.73, f32[2048]{0:T(1024)S(1)} %bitcast.568, bf16[1,4,256,256]{3,2,1,0:T(8,128)(2,1)S(1)} %copy-done.3), kind=kOutput, calls=%fused_computation.5 | convolution fusion | flops 1082130432 | bytes 13115392 | tf_op jit(solution)/shard_map/ikc,ikj->ijc/dot_general | solution.py:32
  293.0 2.5 collective-permute-start
  295.5 90.0 %collective-permute-done = bf16[1024,2048]{1,0:T(8,128)(2,1)} collective-permute-done((bf16[1024,2048]{1,0:T(8,128)(2,1)}, bf16[1024,2048]{1,0:T(8,128)(2,1)}, u32[]{:S(2)}, u32[]{:S(2)}) %collective-permute-start) | collective-permute-done | bytes 4194336 | tf_op jit(solution)/shard_map/ppermute | solution.py:10
  385.5 3.9 broadcast_select_fusion
  389.4 1.9 copy-done.1
  391.3 1.2 fusion.2
  392.5 3.2 copy.21
  395.7 101.9 %all_to_all.47 = bf16[4,256,2048]{2,0,1:T(4,128)(2,1)S(1)} all-to-all(bf16[4,256,2048]{2,0,1:T(4,128)(2,1)S(1)} %copy.21), channel_id=1, replica_groups=mesh['pipe'=4,'seq'=64] {'seq'}, dimensions={1} | all-to-all | bytes 8388608 | tf_op jit(solution)/shard_map/all_to_all | solution.py:25
  497.6 4.1 copy.36
  501.6 6.9 %all_to_all.40 = bf16[256,4,2048]{2,0,1:T(8,128)(2,1)} reshape(bf16[64,4,4,2048]{3,1,0,2:T(4,128)(2,1)} %bitcast.563) | data formatting | bytes 8388608 | tf_op jit(solution)/shard_map/all_to_all | solution.py:25
  508.5 3.5 convert_bitcast_fusion
  553.4 6.0 all-to-all-start.3
  560.2 103.4 %all-reduce.2.cloned.1.call-done = bf16[1024,2048]{1,0:T(8,128)(2,1)} async-done(((bf16[1024,2048]{1,0:T(8,128)(2,1)}), bf16[1024,2048]{1,0:T(8,128)(2,1)}) %all-reduce.2.cloned.1.call-update) | async-done | bytes 4194320 | tf_op jit(solution)/shard_map/psum | solution.py:15
  663.6 2.3 constant_dynamic-slice_fusion
  665.9 10.9 %fusion.3 = bf16[4,256,2048]{2,1,0:T(8,128)(2,1)} fusion(bf16[4,256,2048]{2,1,0:T(8,128)(2,1)} %bitcast.559, bf16[4,256,2048]{2,0,1:T(4,128)(2,1)} %bitcast.147, f32[2048]{0:T(1024)S(1)} %bitcast.569, bf16[1,4,256,256]{3,2,1,0:T(8,128)(2,1)S(1)} %copy-done.3), kind=kOutput, calls=%fused_computation.7 | convolution fusion | flops 1082130432 | bytes 13115392 | tf_op jit(solution)/shard_map/ikc,ikj->ijc/dot_general | solution.py:32
  (142 shorter events, 85.0 us)
Async XLA Ops:
  7.2 127.4 %copy-start = (bf16[1,4,256,256]{3,2,1,0:T(8,128)(2,1)S(1)}, bf16[1,4,256,256]{3,2,1,0:T(8,128)(2,1)}, u32[]{:S(2)}) copy-start(bf16[1,4,256,256]{3,2,1,0:T(8,128)(2,1)} %param.9) | copy-start | bytes 1572868
  180.1 6.9 %copy-start.2 = (bf16[1,2048]{1,0:T(2,128)(2,1)S(1)}, bf16[1,2048]{1,0:T(2,128)(2,1)}, u32[]{:S(2)}) copy-start(bf16[1,2048]{1,0:T(2,128)(2,1)} %param.11) | copy-start | bytes 12292
  180.1 102.0 %copy-start.3 = (bf16[1,4,256,256]{3,2,1,0:T(8,128)(2,1)S(1)}, bf16[1,4,256,256]{3,2,1,0:T(8,128)(2,1)}, u32[]{:S(2)}) copy-start(bf16[1,4,256,256]{3,2,1,0:T(8,128)(2,1)} %param.8) | copy-start | bytes 1572868
  180.1 102.0 %all-to-all-start.1 = ((bf16[64,4,4,2048]{3,1,2,0:T(4,128)(2,1)}), bf16[64,4,4,2048]{3,1,2,0:T(4,128)(2,1)}, u32[]{:S(2)}, u32[]{:S(2)}) async-start(bf16[64,4,4,2048]{3,1,2,0:T(4,128)(2,1)} %constant_dynamic-update-slice_fusion), calls=%async_computation.1 | async-start | bytes 8388608 | tf_op jit(solution)/shard_map/all_to_all | solution.py:30
  186.3 109.2 %all-gather.2.cloned.1.call-start = ((), (), s32[]{:S(2)}) async-start(), calls=%async_computation.4 | async-start | bytes 5242880 | tf_op jit(solution)/shard_map/all_gather | solution.py:40
  293.0 92.5 %collective-permute-start = (bf16[1024,2048]{1,0:T(8,128)(2,1)}, bf16[1024,2048]{1,0:T(8,128)(2,1)}, u32[]{:S(2)}, u32[]{:S(2)}) collective-permute-start(bf16[1024,2048]{1,0:T(8,128)(2,1)} %bitcast.76), channel_id=1, source_target_pairs={{64,0},{128,64},{192,128},{0,192},{65,1},{129,65},{193,129},{1,193... | collective-permute-start | bytes 12582920 | tf_op jit(solution)/shard_map/ppermute | solution.py:10
  389.4 1.9 copy-start.1
  553.4 112.4 %all-to-all-start.3 = ((bf16[64,4,4,2048]{3,1,2,0:T(4,128)(2,1)}), bf16[64,4,4,2048]{3,1,2,0:T(4,128)(2,1)}, u32[]{:S(2)}, u32[]{:S(2)}) async-start(bf16[64,4,4,2048]{3,1,2,0:T(4,128)(2,1)} %constant_dynamic-update-slice_fusion.64), calls=%async_computation.3 | async-start | bytes 8388608 | tf_op jit(solution)/shard_map/all_to_all | solution.py:30
  559.5 104.1 %all-reduce.2.cloned.1.call-start = ((), (), s32[]{:S(2)}) async-start(), calls=%async_computation.5 | async-start | bytes 8388608 | tf_op jit(solution)/shard_map/psum | solution.py:15
Sparse Core Ops, SparseCore 0:
  188.9 51.5 all-gather.1
  563.2 100.3 all-reduce.1
